TPU v7x, 32 devices: a whole 2x2x4 slice. The times are simulated.
32 devices in a mesh: col: 8 (over z, x), row: 4 (over y, core).
Axes of the slice: x: 2, y: 2, z: 4, core: 2. Of those that a mesh axis runs over, the one named last changes fastest.
Arguments:
- position: float32 [128, 16384], P(None, ('col', 'row')), may hold values from -6 to 6
- momentum: float32 [128, 16384], P(None, ('col', 'row')), may hold values from -6 to 6
- row_factors: bfloat16 [16384, 16, 128], P(('col', 'row')), may hold values from -1 to 1
- col_factors: bfloat16 [16384, 16, 128], P(('col', 'row')), may hold values from -1 to 1
- tile_ranks: int32 [16, 16], replicated, may hold values from 16 to 128, as said below
- log_mean: float32 [16384], P(('col', 'row')), may hold values from -0.5 to 0.5
- counts: int32 [16384], P(('col', 'row')), may hold values from 0 to 11
- step_size: float32 [128], replicated, may hold values from 0.1 to 0.3
Outputs:
- new_position: float32 [128, 16384], P(None, ('col', 'row'))
- new_momentum: float32 [128, 16384], P(None, ('col', 'row'))
- energy_change: float32 [128], replicated
Inputs may be any that keep to these rules, and one draw needn't show every extreme that they name: `tile_ranks`: every entry is a multiple of 16; in every draw some tile has rank 16 and some tile has rank 128.
All inputs are finite; a program needn't handle non-finite values.
Results may differ from a plain program's by a relative error of at most 0.004.
Values may be sent and summed in bfloat16 or wider, within the bound.
A program may use at most 128 MiB of HBM per device.

v0:
```python
import jax
import jax.numpy as jnp
from jax import lax
from jax.sharding import PartitionSpec as P


def partner_2(value, axis, stride):
    mask = 2**stride
    pairs = [(source, source ^ mask) for source in range(lax.axis_size(axis))]
    return lax.ppermute(value, axis, pairs)


def on_device(
    position, momentum, row_factors, col_factors, tile_ranks, log_mean, counts, step_size
):
    chains = position.shape[0]
    tile_count = tile_ranks.shape[0]
    ranked = row_factors.shape[2]
    device = lax.axis_index(("col", "row"))
    own_tile = device // 2
    own_half = device % 2
    levels = jnp.arange(ranked, dtype=jnp.int32)
    col_ranks = lax.dynamic_slice_in_dim(tile_ranks, own_tile, 1, 1)[:, 0]
    row_ranks = lax.dynamic_slice_in_dim(tile_ranks, own_tile, 1, 0)[0]
    col_live = (levels[None, :] < col_ranks[:, None]).astype(jnp.float32)[:, :, None]
    row_live = (levels[None, :] < row_ranks[:, None]).astype(jnp.float32)[:, :, None]
    rate_base = counts.astype(jnp.float32)[None, :]

    def deliver(partial_value):
        halved = partial_value.reshape(2 * tile_count, ranked // 2, chains)
        arrived = lax.all_to_all(halved, ("col", "row"), split_axis=0, concat_axis=0, tiled=True)
        summed = arrived.reshape(tile_count, 2, ranked // 2, chains).astype(jnp.float32).sum(axis=1)
        summed = summed.astype(jnp.bfloat16)
        partner = partner_2(summed, "row", 0)
        lower_first = jnp.concatenate([summed, partner], axis=1)
        upper_first = jnp.concatenate([partner, summed], axis=1)
        return jnp.where(own_half == 0, lower_first, upper_first)

    def gradient(values):
        rounded = values.astype(jnp.bfloat16)
        partial_value = jnp.einsum(
            "yik,hy->ikh", col_factors, rounded, preferred_element_type=jnp.float32
        )
        partial_value = (partial_value * col_live).astype(jnp.bfloat16)
        coefficient = deliver(partial_value)
        latent_field = jnp.einsum(
            "xjk,jkh->hx", row_factors, coefficient, preferred_element_type=jnp.float32
        )
        exponent = log_mean[None, :] + latent_field
        intensity = jnp.exp(exponent)
        residual = rate_base - intensity
        adjoint = jnp.einsum(
            "xjk,hx->jkh",
            row_factors,
            residual.astype(jnp.bfloat16),
            preferred_element_type=jnp.float32,
        )
        adjoint = (adjoint * row_live).astype(jnp.bfloat16)
        returned = deliver(adjoint)
        pulled = jnp.einsum(
            "yik,ikh->hy", col_factors, returned, preferred_element_type=jnp.float32
        )
        energy = jnp.sum(intensity - rate_base * exponent + 0.5 * values * values, axis=1)
        return (values - pulled, energy)

    full_step = step_size[:, None]

    def leapfrog(section, carry):
        shifted, moment, start_energy, end_energy = carry
        forces, energy = gradient(shifted)
        weight = jnp.where(section == 1, 1.0, 0.5).astype(jnp.float32)
        moment = moment - weight * full_step * forces
        advance = jnp.where(section < 2, full_step * moment, jnp.zeros_like(moment))
        shifted = shifted + advance
        start_energy = jnp.where(section == 0, energy, start_energy)
        end_energy = jnp.where(section == 2, energy, end_energy)
        return (shifted, moment, start_energy, end_energy)

    empty = jnp.zeros((chains,), jnp.float32)
    shifted, moment, start_energy, end_energy = lax.fori_loop(
        0, 3, leapfrog, (position, momentum, empty, empty)
    )
    kinetic = 0.5 * jnp.sum(moment * moment - momentum * momentum, axis=1)
    change = lax.psum(end_energy - start_energy + kinetic, ("col", "row"))
    return (shifted, moment, change)


def solution(mesh):
    in_specs = (
        P(None, ("col", "row")),
        P(None, ("col", "row")),
        P(("col", "row"), None, None),
        P(("col", "row"), None, None),
        P(),
        P(("col", "row")),
        P(("col", "row")),
        P(),
    )
    out_specs = (P(None, ("col", "row")), P(None, ("col", "row")), P())
    return jax.shard_map(
        on_device, mesh=mesh, in_specs=in_specs, out_specs=out_specs, check_vma=False
    )
```

profile of v0, /device:TPU:0, one launch (start us, length us, event | category | flops | bytes accessed | tf_op | source)
XLA Modules:
  0.0 186.0 jit_solution(8267048132765236905)
XLA Ops:
  0.7 0.7 copy-done
  1.5 2.1 %copy.23 = bf16[512,16,128]{2,0,1:T(8,128)(2,1)S(1)} copy(bf16[512,16,128]{2,1,0:T(8,128)(2,1)} %param.13) | data formatting | bytes 4194304
  3.7 4.4 %copy.24 = bf16[512,16,128]{0,2,1:T(8,128)(2,1)} copy(bf16[512,16,128]{2,1,0:T(8,128)(2,1)} %param.12) | data formatting | bytes 4194304
  8.2 138.8 %while.23 = (s32[]{:T(128)}, f32[128,512]{1,0:T(8,128)S(1)}, f32[128,512]{1,0:T(8,128)S(1)}, f32[128]{0:T(128)S(1)}, f32[128]{0:T(128)S(1)}, /*index=5*/f32[128,...) while((s32[]{:T(128)}, f32[128,512]{1,0:T(8,128)S(1)}, ...), condition=%wide.region_4.5_spmd.clone, body=%wide.region_0.4_spmd.clone.sunk | while | flops 1080828416 | bytes 28880336 | solution.py:80
  8.3 0.9 fusion.47
  9.2 22.7 %all_to_all.30 = bf16[32,64,128]{2,1,0:T(8,128)(2,1)S(1)} all-to-all(bf16[32,64,128]{2,1,0:T(8,128)(2,1)S(1)} %bitcast.77), channel_id=1, replica_groups=mesh['col'=8,'row'=4] {'col','row'}, dimensions={0} | all-to-all | bytes 1048576 | tf_op jit(solution)/shard_map/while/body/eval_jaxpr/all_to_all | solution.py:31
  32.1 1.4 collective-permute-done
  33.6 0.5 fusion.48
  34.1 0.7 fusion.49
  34.8 0.3 multiply_convert_fusion.2
  35.1 18.4 %all_to_all.31 = bf16[32,64,128]{2,1,0:T(8,128)(2,1)S(1)} all-to-all(bf16[32,64,128]{2,1,0:T(8,128)(2,1)S(1)} %bitcast.76), channel_id=1, replica_groups=mesh['col'=8,'row'=4] {'col','row'}, dimensions={0} | all-to-all | bytes 1048576 | tf_op jit(solution)/shard_map/while/body/eval_jaxpr/all_to_all | solution.py:31
  53.7 1.6 collective-permute-done.1
  55.4 2.0 %fusion.50 = (f32[128]{0:T(128)S(1)}, f32[128,512]{1,0:T(8,128)S(1)}, f32[128,512]{1,0:T(8,128)S(1)}) fusion(f32[128,512]{1,0:T(8,128)S(1)} %get-tuple-element.580, f32[128,512]{1,0:T(8,128)S(1)} %fusion.48, f32[512]{0:T(512)S(1)} %bitcast.80, f32[128]{0:T(128)S(1)} %bitcast.82, pred[]{:T(512)S(6)} %lt.137, f32[128,512]{1,0:T(8,128)S(1)} %get-tuple-element.581, ...), kind=kOutput, calls=%fused_computation.29.clone.1 | convolution fusion | flops 271581056 | bytes 3935746 | tf_op jit(solution)/shard_map/while/body/eval_jaxpr/yik,ikh->hy/dot_general | solution.py:60
  57.4 0.9 fusion.47
  58.3 18.4 %all_to_all.30 = bf16[32,64,128]{2,1,0:T(8,128)(2,1)S(1)} all-to-all(bf16[32,64,128]{2,1,0:T(8,128)(2,1)S(1)} %bitcast.77), channel_id=1, replica_groups=mesh['col'=8,'row'=4] {'col','row'}, dimensions={0} | all-to-all | bytes 1048576 | tf_op jit(solution)/shard_map/while/body/eval_jaxpr/all_to_all | solution.py:31
  77.0 1.4 collective-permute-done
  78.4 0.5 fusion.48
  78.9 0.7 fusion.49
  79.6 0.3 multiply_convert_fusion.2
  80.0 18.4 %all_to_all.31 = bf16[32,64,128]{2,1,0:T(8,128)(2,1)S(1)} all-to-all(bf16[32,64,128]{2,1,0:T(8,128)(2,1)S(1)} %bitcast.76), channel_id=1, replica_groups=mesh['col'=8,'row'=4] {'col','row'}, dimensions={0} | all-to-all | bytes 1048576 | tf_op jit(solution)/shard_map/while/body/eval_jaxpr/all_to_all | solution.py:31
  98.5 1.6 collective-permute-done.1
  100.2 1.9 %fusion.50 = (f32[128]{0:T(128)S(1)}, f32[128,512]{1,0:T(8,128)S(1)}, f32[128,512]{1,0:T(8,128)S(1)}) fusion(f32[128,512]{1,0:T(8,128)S(1)} %get-tuple-element.580, f32[128,512]{1,0:T(8,128)S(1)} %fusion.48, f32[512]{0:T(512)S(1)} %bitcast.80, f32[128]{0:T(128)S(1)} %bitcast.82, pred[]{:T(512)S(6)} %lt.137, f32[128,512]{1,0:T(8,128)S(1)} %get-tuple-element.581, ...), kind=kOutput, calls=%fused_computation.29.clone.1 | convolution fusion | flops 271581056 | bytes 3935746 | tf_op jit(solution)/shard_map/while/body/eval_jaxpr/yik,ikh->hy/dot_general | solution.py:60
  102.2 0.9 fusion.47
  103.2 18.4 %all_to_all.30 = bf16[32,64,128]{2,1,0:T(8,128)(2,1)S(1)} all-to-all(bf16[32,64,128]{2,1,0:T(8,128)(2,1)S(1)} %bitcast.77), channel_id=1, replica_groups=mesh['col'=8,'row'=4] {'col','row'}, dimensions={0} | all-to-all | bytes 1048576 | tf_op jit(solution)/shard_map/while/body/eval_jaxpr/all_to_all | solution.py:31
  121.8 1.4 collective-permute-done
  123.2 0.5 fusion.48
  123.7 0.7 fusion.49
  124.4 0.3 multiply_convert_fusion.2
  124.8 18.4 %all_to_all.31 = bf16[32,64,128]{2,1,0:T(8,128)(2,1)S(1)} all-to-all(bf16[32,64,128]{2,1,0:T(8,128)(2,1)S(1)} %bitcast.76), channel_id=1, replica_groups=mesh['col'=8,'row'=4] {'col','row'}, dimensions={0} | all-to-all | bytes 1048576 | tf_op jit(solution)/shard_map/while/body/eval_jaxpr/all_to_all | solution.py:31
  143.4 1.6 collective-permute-done.1
  145.0 2.0 %fusion.50 = (f32[128]{0:T(128)S(1)}, f32[128,512]{1,0:T(8,128)S(1)}, f32[128,512]{1,0:T(8,128)S(1)}) fusion(f32[128,512]{1,0:T(8,128)S(1)} %get-tuple-element.580, f32[128,512]{1,0:T(8,128)S(1)} %fusion.48, f32[512]{0:T(512)S(1)} %bitcast.80, f32[128]{0:T(128)S(1)} %bitcast.82, pred[]{:T(512)S(6)} %lt.137, f32[128,512]{1,0:T(8,128)S(1)} %get-tuple-element.581, ...), kind=kOutput, calls=%fused_computation.29.clone.1 | convolution fusion | flops 271581056 | bytes 3935746 | tf_op jit(solution)/shard_map/while/body/eval_jaxpr/yik,ikh->hy/dot_general | solution.py:60
  147.1 38.9 %psum.7 = f32[128]{0:T(128)} all-reduce(f32[128]{0:T(128)S(1)} %multiply_add_fusion), channel_id=1, replica_groups=mesh['col'=8,'row'=4] {'col','row'}, use_global_device_ids=true, to_apply=%region_6.7 | all-reduce | flops 128 | bytes 1024 | tf_op jit(solution)/shard_map/psum | solution.py:84
  (54 shorter events, 1.8 us)
Async XLA Ops:
  0.6 0.7 copy-start
  3.7 4.4 %copy-start.7 = (s32[512]{0:T(512)S(1)}, s32[512]{0:T(512)}, u32[]{:S(2)}) copy-start(s32[512]{0:T(512)} %param.16) | copy-start | bytes 6148
  3.7 4.4 %copy-start.3 = (f32[128,512]{1,0:T(8,128)S(1)}, f32[128,512]{1,0:T(8,128)}, u32[]{:S(2)}) copy-start(f32[128,512]{1,0:T(8,128)} %param.10) | copy-start | bytes 786436
  3.7 4.4 %copy-start.6 = (f32[128,512]{1,0:T(8,128)S(1)}, f32[128,512]{1,0:T(8,128)}, u32[]{:S(2)}) copy-start(f32[128,512]{1,0:T(8,128)} %param.11) | copy-start | bytes 786436
  3.7 4.4 %copy-start.8 = (f32[512]{0:T(512)S(1)}, f32[512]{0:T(512)}, u32[]{:S(2)}) copy-start(f32[512]{0:T(512)} %param.15) | copy-start | bytes 6148
  3.7 4.4 %copy-start.9 = (f32[128]{0:T(128)S(1)}, f32[128]{0:T(128)}, u32[]{:S(2)}) copy-start(f32[128]{0:T(128)} %param.17) | copy-start | bytes 1540
  8.2 138.9 %copy-start.4 = (f32[128,512]{1,0:T(8,128)S(1)}, f32[128,512]{1,0:T(8,128)}, u32[]{:S(2)}) copy-start(f32[128,512]{1,0:T(8,128)} %param.11) | copy-start | bytes 786436
  8.3 25.4 %copy-start.1 = (bf16[512,16,128]{0,2,1:T(8,128)(2,1)S(1)}, bf16[512,16,128]{0,2,1:T(8,128)(2,1)}, u32[]{:S(2)}) copy-start(bf16[512,16,128]{0,2,1:T(8,128)(2,1)} %get-tuple-element.607) | copy-start | bytes 6291460 | tf_op jit(solution)/shard_map/while
  32.0 1.6 collective-permute-start
  53.6 1.7 collective-permute-start.1
  57.4 21.0 %copy-start.1 = (bf16[512,16,128]{0,2,1:T(8,128)(2,1)S(1)}, bf16[512,16,128]{0,2,1:T(8,128)(2,1)}, u32[]{:S(2)}) copy-start(bf16[512,16,128]{0,2,1:T(8,128)(2,1)} %get-tuple-element.607) | copy-start | bytes 6291460 | tf_op jit(solution)/shard_map/while
  76.8 1.6 collective-permute-start
  98.4 1.7 collective-permute-start.1
  102.2 21.0 %copy-start.1 = (bf16[512,16,128]{0,2,1:T(8,128)(2,1)S(1)}, bf16[512,16,128]{0,2,1:T(8,128)(2,1)}, u32[]{:S(2)}) copy-start(bf16[512,16,128]{0,2,1:T(8,128)(2,1)} %get-tuple-element.607) | copy-start | bytes 6291460 | tf_op jit(solution)/shard_map/while
  121.6 1.6 collective-permute-start
  143.3 1.7 collective-permute-start.1
  147.0 39.1 %copy-start.2 = (f32[128,512]{1,0:T(8,128)}, f32[128,512]{1,0:T(8,128)S(1)}, u32[]{:S(2)}) copy-start(f32[128,512]{1,0:T(8,128)S(1)} %get-tuple-element.347) | copy-start | bytes 786436
  147.0 39.0 %copy-start.5 = (f32[128,512]{1,0:T(8,128)}, f32[128,512]{1,0:T(8,128)S(1)}, u32[]{:S(2)}) copy-start(f32[128,512]{1,0:T(8,128)S(1)} %get-tuple-element.348) | copy-start | bytes 786436
where the time goes:
time: 187 us; the launch traced here: 186 us
  blocking collectives  154 us (82%)
  matrix products  12.1 us (6%)
  waiting for transfers between devices  9.24 us (5%)
  local copies, waits for them, and re-layouts  7.44 us (4%)
  other arithmetic  2.09 us (1%)
    all_to_all x6, blocking collectives, deliver(): lax.all_to_all(halved, ('col', 'row'), split_axis=0, concat_axis=0, tiled...  115 us
    psum x1, blocking collectives, on_device(): change = lax.psum(end_energy - start_energy + kinetic, ('col', 'row'))  38.9 us
    ppermute x6, waiting for transfers between devices, partner_2(): return lax.ppermute(value, axis, pairs)  9.24 us
    unnamed x20, local copies, waits for them, and re-layouts  7.24 us
    dot_general x3, matrix products, gradient(): jnp.einsum('yik,ikh->hy', col_factors, returned, preferred_element_type=j...  5.85 us
  transfers between devices with their start and end apart: 6, of which 6 were waited for; matrix products, arithmetic and copies ran while one was open for 0% of the time, Pallas kernels for 0%

commit v1 on v0

--- a/solution.py
+++ b/solution.py
@@ -81,7 +81,8 @@
         0, 3, leapfrog, (position, momentum, empty, empty)
     )
     kinetic = 0.5 * jnp.sum(moment * moment - momentum * momentum, axis=1)
-    change = lax.psum(end_energy - start_energy + kinetic, ("col", "row"))
+    partial = lax.psum(end_energy - start_energy + kinetic, "col")
+    change = lax.psum(partial, "row")
     return (shifted, moment, change)
 
 

time: 187 us -> 173 us (0.925)
  blocking collectives: 154 us -> 140 us
    psum x1 -> x2, blocking collectives: 38.9 us -> 25 us  [the longest x1 18.8 us: on_device(): partial = lax.psum(end_energy - start_energy + kinetic, 'col')]
where the time goes in v1:
time: 173 us; the launch traced here: 172 us
  blocking collectives  140 us (81%)
  matrix products  12.1 us (7%)
  waiting for transfers between devices  9.24 us (5%)
  local copies, waits for them, and re-layouts  7.44 us (4%)
  other arithmetic  2.09 us (1%)
    all_to_all x6, blocking collectives, deliver(): lax.all_to_all(halved, ('col', 'row'), split_axis=0, concat_axis=0, tiled...  115 us
    psum x1, blocking collectives, on_device(): partial = lax.psum(end_energy - start_energy + kinetic, 'col')  18.8 us
    ppermute x6, waiting for transfers between devices, partner_2(): return lax.ppermute(value, axis, pairs)  9.24 us
    unnamed x20, local copies, waits for them, and re-layouts  7.24 us
    psum x1, blocking collectives, on_device(): change = lax.psum(partial, 'row')  6.15 us
    dot_general x3, matrix products, gradient(): jnp.einsum('yik,ikh->hy', col_factors, returned, preferred_element_type=j...  5.85 us
  transfers between devices with their start and end apart: 6, of which 6 were waited for; matrix products, arithmetic and copies ran while one was open for 0% of the time, Pallas kernels for 0%

profile of v1, /device:TPU:0, one launch (start us, length us, event | category | flops | bytes accessed | tf_op | source)
XLA Modules:
  0.0 172.1 jit_solution(13073980350378877076)
XLA Ops:
  0.7 0.7 copy-done
  1.5 2.1 %copy.23 = bf16[512,16,128]{2,0,1:T(8,128)(2,1)S(1)} copy(bf16[512,16,128]{2,1,0:T(8,128)(2,1)} %param.13) | data formatting | bytes 4194304
  3.7 4.4 %copy.24 = bf16[512,16,128]{0,2,1:T(8,128)(2,1)} copy(bf16[512,16,128]{2,1,0:T(8,128)(2,1)} %param.12) | data formatting | bytes 4194304
  8.2 138.8 %while.23 = (s32[]{:T(128)}, f32[128,512]{1,0:T(8,128)S(1)}, f32[128,512]{1,0:T(8,128)S(1)}, f32[128]{0:T(128)S(1)}, f32[128]{0:T(128)S(1)}, /*index=5*/f32[128,...) while((s32[]{:T(128)}, f32[128,512]{1,0:T(8,128)S(1)}, ...), condition=%wide.region_4.5_spmd.clone, body=%wide.region_0.4_spmd.clone.sunk | while | flops 1080828416 | bytes 28880336 | solution.py:80
  8.3 0.9 fusion.47
  9.2 22.7 %all_to_all.30 = bf16[32,64,128]{2,1,0:T(8,128)(2,1)S(1)} all-to-all(bf16[32,64,128]{2,1,0:T(8,128)(2,1)S(1)} %bitcast.77), channel_id=1, replica_groups=mesh['col'=8,'row'=4] {'col','row'}, dimensions={0} | all-to-all | bytes 1048576 | tf_op jit(solution)/shard_map/while/body/eval_jaxpr/all_to_all | solution.py:31
  32.1 1.4 collective-permute-done
  33.6 0.5 fusion.48
  34.1 0.7 fusion.49
  34.8 0.3 multiply_convert_fusion.2
  35.1 18.4 %all_to_all.31 = bf16[32,64,128]{2,1,0:T(8,128)(2,1)S(1)} all-to-all(bf16[32,64,128]{2,1,0:T(8,128)(2,1)S(1)} %bitcast.76), channel_id=1, replica_groups=mesh['col'=8,'row'=4] {'col','row'}, dimensions={0} | all-to-all | bytes 1048576 | tf_op jit(solution)/shard_map/while/body/eval_jaxpr/all_to_all | solution.py:31
  53.7 1.6 collective-permute-done.1
  55.4 2.0 %fusion.50 = (f32[128]{0:T(128)S(1)}, f32[128,512]{1,0:T(8,128)S(1)}, f32[128,512]{1,0:T(8,128)S(1)}) fusion(f32[128,512]{1,0:T(8,128)S(1)} %get-tuple-element.580, f32[128,512]{1,0:T(8,128)S(1)} %fusion.48, f32[512]{0:T(512)S(1)} %bitcast.80, f32[128]{0:T(128)S(1)} %bitcast.82, pred[]{:T(512)S(6)} %lt.137, f32[128,512]{1,0:T(8,128)S(1)} %get-tuple-element.581, ...), kind=kOutput, calls=%fused_computation.29.clone.1 | convolution fusion | flops 271581056 | bytes 3935746 | tf_op jit(solution)/shard_map/while/body/eval_jaxpr/yik,ikh->hy/dot_general | solution.py:60
  57.4 0.9 fusion.47
  58.3 18.4 %all_to_all.30 = bf16[32,64,128]{2,1,0:T(8,128)(2,1)S(1)} all-to-all(bf16[32,64,128]{2,1,0:T(8,128)(2,1)S(1)} %bitcast.77), channel_id=1, replica_groups=mesh['col'=8,'row'=4] {'col','row'}, dimensions={0} | all-to-all | bytes 1048576 | tf_op jit(solution)/shard_map/while/body/eval_jaxpr/all_to_all | solution.py:31
  77.0 1.4 collective-permute-done
  78.4 0.5 fusion.48
  78.9 0.7 fusion.49
  79.6 0.3 multiply_convert_fusion.2
  80.0 18.4 %all_to_all.31 = bf16[32,64,128]{2,1,0:T(8,128)(2,1)S(1)} all-to-all(bf16[32,64,128]{2,1,0:T(8,128)(2,1)S(1)} %bitcast.76), channel_id=1, replica_groups=mesh['col'=8,'row'=4] {'col','row'}, dimensions={0} | all-to-all | bytes 1048576 | tf_op jit(solution)/shard_map/while/body/eval_jaxpr/all_to_all | solution.py:31
  98.5 1.6 collective-permute-done.1
  100.2 1.9 %fusion.50 = (f32[128]{0:T(128)S(1)}, f32[128,512]{1,0:T(8,128)S(1)}, f32[128,512]{1,0:T(8,128)S(1)}) fusion(f32[128,512]{1,0:T(8,128)S(1)} %get-tuple-element.580, f32[128,512]{1,0:T(8,128)S(1)} %fusion.48, f32[512]{0:T(512)S(1)} %bitcast.80, f32[128]{0:T(128)S(1)} %bitcast.82, pred[]{:T(512)S(6)} %lt.137, f32[128,512]{1,0:T(8,128)S(1)} %get-tuple-element.581, ...), kind=kOutput, calls=%fused_computation.29.clone.1 | convolution fusion | flops 271581056 | bytes 3935746 | tf_op jit(solution)/shard_map/while/body/eval_jaxpr/yik,ikh->hy/dot_general | solution.py:60
  102.2 0.9 fusion.47
  103.2 18.4 %all_to_all.30 = bf16[32,64,128]{2,1,0:T(8,128)(2,1)S(1)} all-to-all(bf16[32,64,128]{2,1,0:T(8,128)(2,1)S(1)} %bitcast.77), channel_id=1, replica_groups=mesh['col'=8,'row'=4] {'col','row'}, dimensions={0} | all-to-all | bytes 1048576 | tf_op jit(solution)/shard_map/while/body/eval_jaxpr/all_to_all | solution.py:31
  121.8 1.4 collective-permute-done
  123.2 0.5 fusion.48
  123.7 0.7 fusion.49
  124.8 18.4 %all_to_all.31 = bf16[32,64,128]{2,1,0:T(8,128)(2,1)S(1)} all-to-all(bf16[32,64,128]{2,1,0:T(8,128)(2,1)S(1)} %bitcast.76), channel_id=1, replica_groups=mesh['col'=8,'row'=4] {'col','row'}, dimensions={0} | all-to-all | bytes 1048576 | tf_op jit(solution)/shard_map/while/body/eval_jaxpr/all_to_all | solution.py:31
  143.4 1.6 collective-permute-done.1
  145.0 2.0 %fusion.50 = (f32[128]{0:T(128)S(1)}, f32[128,512]{1,0:T(8,128)S(1)}, f32[128,512]{1,0:T(8,128)S(1)}) fusion(f32[128,512]{1,0:T(8,128)S(1)} %get-tuple-element.580, f32[128,512]{1,0:T(8,128)S(1)} %fusion.48, f32[512]{0:T(512)S(1)} %bitcast.80, f32[128]{0:T(128)S(1)} %bitcast.82, pred[]{:T(512)S(6)} %lt.137, f32[128,512]{1,0:T(8,128)S(1)} %get-tuple-element.581, ...), kind=kOutput, calls=%fused_computation.29.clone.1 | convolution fusion | flops 271581056 | bytes 3935746 | tf_op jit(solution)/shard_map/while/body/eval_jaxpr/yik,ikh->hy/dot_general | solution.py:60
  147.1 18.8 %psum.14 = f32[128]{0:T(128)S(1)} all-reduce(f32[128]{0:T(128)S(1)} %multiply_add_fusion), channel_id=1, replica_groups=mesh['col'=8,'row'=4] {'col'}, use_global_device_ids=true, to_apply=%region_6.7 | all-reduce | flops 128 | bytes 1024 | tf_op jit(solution)/shard_map/psum | solution.py:84
  166.0 6.2 %psum.15 = f32[128]{0:T(128)} all-reduce(f32[128]{0:T(128)S(1)} %psum.14), channel_id=1, replica_groups=mesh['col'=8,'row'=4] {'row'}, use_global_device_ids=true, to_apply=%region_7.8 | all-reduce | flops 128 | bytes 1024 | tf_op jit(solution)/shard_map/psum | solution.py:85
  (55 shorter events, 2.1 us)
Async XLA Ops:
  0.6 0.7 copy-start
  3.7 4.4 %copy-start.7 = (s32[512]{0:T(512)S(1)}, s32[512]{0:T(512)}, u32[]{:S(2)}) copy-start(s32[512]{0:T(512)} %param.16) | copy-start | bytes 6148
  3.7 4.4 %copy-start.3 = (f32[128,512]{1,0:T(8,128)S(1)}, f32[128,512]{1,0:T(8,128)}, u32[]{:S(2)}) copy-start(f32[128,512]{1,0:T(8,128)} %param.10) | copy-start | bytes 786436
  3.7 4.4 %copy-start.6 = (f32[128,512]{1,0:T(8,128)S(1)}, f32[128,512]{1,0:T(8,128)}, u32[]{:S(2)}) copy-start(f32[128,512]{1,0:T(8,128)} %param.11) | copy-start | bytes 786436
  3.7 4.4 %copy-start.8 = (f32[512]{0:T(512)S(1)}, f32[512]{0:T(512)}, u32[]{:S(2)}) copy-start(f32[512]{0:T(512)} %param.15) | copy-start | bytes 6148
  3.7 4.4 %copy-start.9 = (f32[128]{0:T(128)S(1)}, f32[128]{0:T(128)}, u32[]{:S(2)}) copy-start(f32[128]{0:T(128)} %param.17) | copy-start | bytes 1540
  8.2 138.9 %copy-start.4 = (f32[128,512]{1,0:T(8,128)S(1)}, f32[128,512]{1,0:T(8,128)}, u32[]{:S(2)}) copy-start(f32[128,512]{1,0:T(8,128)} %param.11) | copy-start | bytes 786436
  8.3 25.4 %copy-start.1 = (bf16[512,16,128]{0,2,1:T(8,128)(2,1)S(1)}, bf16[512,16,128]{0,2,1:T(8,128)(2,1)}, u32[]{:S(2)}) copy-start(bf16[512,16,128]{0,2,1:T(8,128)(2,1)} %get-tuple-element.607) | copy-start | bytes 6291460 | tf_op jit(solution)/shard_map/while
  32.0 1.6 collective-permute-start
  53.6 1.7 %collective-permute-start.1 = (bf16[16,64,128]{2,1,0:T(8,128)(2,1)S(1)}, bf16[16,64,128]{2,1,0:T(8,128)(2,1)}, u32[]{:S(2)}, u32[]{:S(2)}) collective-permute-start(bf16[16,64,128]{2,1,0:T(8,128)(2,1)S(1)} %bitcast_reduce_fusion.5), channel_id=1, source_target_pairs={{0,1},{1,0},{2,3},{3,2},{4,5},{5,4},{6,7},{7,6},{8,9},{9,8},{10,11... | collective-permute-start | bytes 786440 | tf_op jit(solution)/shard_map/while/body/eval_jaxpr/ppermute | solution.py:10
  57.4 21.0 %copy-start.1 = (bf16[512,16,128]{0,2,1:T(8,128)(2,1)S(1)}, bf16[512,16,128]{0,2,1:T(8,128)(2,1)}, u32[]{:S(2)}) copy-start(bf16[512,16,128]{0,2,1:T(8,128)(2,1)} %get-tuple-element.607) | copy-start | bytes 6291460 | tf_op jit(solution)/shard_map/while
  76.8 1.6 collective-permute-start
  98.4 1.7 %collective-permute-start.1 = (bf16[16,64,128]{2,1,0:T(8,128)(2,1)S(1)}, bf16[16,64,128]{2,1,0:T(8,128)(2,1)}, u32[]{:S(2)}, u32[]{:S(2)}) collective-permute-start(bf16[16,64,128]{2,1,0:T(8,128)(2,1)S(1)} %bitcast_reduce_fusion.5), channel_id=1, source_target_pairs={{0,1},{1,0},{2,3},{3,2},{4,5},{5,4},{6,7},{7,6},{8,9},{9,8},{10,11... | collective-permute-start | bytes 786440 | tf_op jit(solution)/shard_map/while/body/eval_jaxpr/ppermute | solution.py:10
  102.2 21.0 %copy-start.1 = (bf16[512,16,128]{0,2,1:T(8,128)(2,1)S(1)}, bf16[512,16,128]{0,2,1:T(8,128)(2,1)}, u32[]{:S(2)}) copy-start(bf16[512,16,128]{0,2,1:T(8,128)(2,1)} %get-tuple-element.607) | copy-start | bytes 6291460 | tf_op jit(solution)/shard_map/while
  121.6 1.6 collective-permute-start
  143.3 1.7 %collective-permute-start.1 = (bf16[16,64,128]{2,1,0:T(8,128)(2,1)S(1)}, bf16[16,64,128]{2,1,0:T(8,128)(2,1)}, u32[]{:S(2)}, u32[]{:S(2)}) collective-permute-start(bf16[16,64,128]{2,1,0:T(8,128)(2,1)S(1)} %bitcast_reduce_fusion.5), channel_id=1, source_target_pairs={{0,1},{1,0},{2,3},{3,2},{4,5},{5,4},{6,7},{7,6},{8,9},{9,8},{10,11... | collective-permute-start | bytes 786440 | tf_op jit(solution)/shard_map/while/body/eval_jaxpr/ppermute | solution.py:10
  147.0 25.1 %copy-start.2 = (f32[128,512]{1,0:T(8,128)}, f32[128,512]{1,0:T(8,128)S(1)}, u32[]{:S(2)}) copy-start(f32[128,512]{1,0:T(8,128)S(1)} %get-tuple-element.347) | copy-start | bytes 786436
  147.0 25.1 %copy-start.5 = (f32[128,512]{1,0:T(8,128)}, f32[128,512]{1,0:T(8,128)S(1)}, u32[]{:S(2)}) copy-start(f32[128,512]{1,0:T(8,128)S(1)} %get-tuple-element.348) | copy-start | bytes 786436
